TPU v7x, 32 devices: a whole 2x2x4 slice. The times are simulated.
32 devices in a mesh: groups: 2 (over x), space: 16 (over z, y, core).
Axes of the slice: x: 2, y: 2, z: 4, core: 2. Of those that a mesh axis runs over, the one named last changes fastest.
Arguments:
- noisy: bfloat16 [16384, 512], P(('groups', 'space')), parts along dimension 0, may hold values from -6 to 6
- matches: int32 [3072, 16], P(('groups', 'space')), parts along dimension 0, may hold values from 0 to 8191, as said below
- cube_home: int32 [16384], P('groups'), parts along dimension 0, may hold values from 0 to 8191, as said below
- sigma_coef: float32 [512], replicated, may hold values from 0.3 to 1.5
Outputs:
- basic: bfloat16 [16384, 512], P(('groups', 'space')), parts along dimension 0
- final: bfloat16 [16384, 512], P(('groups', 'space')), parts along dimension 0
There are 2 independent parts, one for each index of `groups`. A program takes and returns all parts, laid end to end along the dimension named above; an argument that names none is the same for every part. Nothing has to cross between parts.
Inputs may be any that keep to these rules, and one draw needn't show every extreme that they name: `matches`: each device's 16 * 96 list entries name at most 192 cubes whose table rows lie in any one device's block of 512 rows; in every draw one block receives exactly 192 from every device. `cube_home`: A permutation of the table rows.
All inputs are finite; a program needn't handle non-finite values.
Results may differ from a plain program's by a relative error of at most 0.0079.
Values may be sent and summed in bfloat16 or wider, within the bound.
A program may use at most 64 MiB of HBM per device.

v0:
```python
import jax
import jax.numpy as jnp
from jax import lax
from jax.sharding import PartitionSpec as P

shrink_level = 2.7
prior_weight = 0.5


def dct_matrix(length):
    index = jnp.arange(length, dtype=jnp.float32)
    freq = index[:, None]
    table = jnp.cos(jnp.pi * (2.0 * index[None, :] + 1.0) * freq / (2.0 * length)) * jnp.sqrt(
        2.0 / length
    )
    return jnp.where(freq == 0, table / jnp.sqrt(2.0), table)


def make_tables(group):
    small = dct_matrix(8)
    cube_table = (
        jnp.einsum("ad,be,cf->abcdef", small, small, small).reshape(512, 512).astype(jnp.bfloat16)
    )
    return (cube_table, dct_matrix(group))


def cube_spectra(rows_in, cube_table):
    return jnp.dot(rows_in, cube_table.T, preferred_element_type=jnp.float32)


def group_mix(spec, group_table):
    return jnp.einsum("jm,rmk->rjk", group_table, spec, precision=lax.Precision.HIGHEST)


def forward(members, cube_table, group_table):
    spec = cube_spectra(members.reshape(-1, members.shape[-1]), cube_table).reshape(members.shape)
    return group_mix(spec, group_table)


def backward(coeffs, cube_table, group_table):
    back = jnp.einsum("jm,rjk->rmk", group_table, coeffs, precision=lax.Precision.HIGHEST).astype(
        jnp.bfloat16
    )
    out = jnp.dot(back.reshape(-1, back.shape[-1]), cube_table, preferred_element_type=jnp.float32)
    return out.reshape(coeffs.shape)


def aggregate(parts, weights, targets, noisy, count):
    numer = jax.ops.segment_sum(parts.astype(jnp.float32), targets, count)
    denom = jax.ops.segment_sum(weights.astype(jnp.float32), targets, count)
    return (
        (numer + prior_weight * noisy.astype(jnp.float32)) / (denom[:, None] + prior_weight)
    ).astype(jnp.bfloat16)


def first_phase(coeffs, sigma_coef, cube_table, group_table):
    level = (shrink_level * sigma_coef) ** 2
    square = coeffs * coeffs
    gain = square / (square + level)
    weight = 1.0 / (0.25 + jnp.mean(gain * gain, axis=(1, 2)))
    out = backward(gain * coeffs, cube_table, group_table)
    part = (weight[:, None, None] * out).astype(jnp.bfloat16)
    wcopy = jnp.broadcast_to(weight[:, None], out.shape[:2]).astype(jnp.bfloat16)
    return (part, wcopy)


def second_phase(coeffs, gcoeffs, sigma_coef, cube_table, group_table):
    noise = sigma_coef * sigma_coef
    square = gcoeffs * gcoeffs
    wiener = square / (square + noise)
    weight = 1.0 / (0.25 + jnp.mean(wiener * wiener * noise, axis=(1, 2)))
    out = backward(wiener * coeffs, cube_table, group_table)
    part = (weight[:, None, None] * out).astype(jnp.bfloat16)
    wcopy = jnp.broadcast_to(weight[:, None], out.shape[:2]).astype(jnp.bfloat16)
    return (part, wcopy)


def pack_slots(part, wcopy, place, count, slots):
    width = part.shape[-1]
    entries = place.shape[0]
    buffer = (
        jnp.zeros((count * slots, width), jnp.bfloat16).at[place].set(part.reshape(entries, width))
    )
    wbuffer = jnp.zeros((count * slots,), jnp.bfloat16).at[place].set(wcopy.reshape(entries))
    return (buffer.reshape(count, slots, width), wbuffer.reshape(count, slots))


def body(noisy, matches, cube_home, sigma_coef):
    cube_table, group_table = make_tables(matches.shape[1])
    count = lax.axis_size("space")
    refs, group = matches.shape
    entries = refs * group
    slots = 2 * entries // count
    rows_here = noisy.shape[0]
    width = noisy.shape[1]
    table_row = cube_home[matches.reshape(-1)]
    owner = table_row // rows_here
    local = table_row % rows_here
    onehot = (owner[:, None] == jnp.arange(count, dtype=jnp.int32)[None, :]).astype(jnp.int32)
    ranks = jnp.cumsum(onehot, axis=0) - 1
    slot = jnp.sum(ranks * onehot, axis=1)
    place = owner * slots + slot
    request = jnp.zeros((count * slots,), jnp.int32).at[place].set(local).reshape(count, slots)
    asked = lax.all_to_all(request, "space", split_axis=0, concat_axis=0, tiled=True)
    asked_flat = asked.reshape(-1)
    served = noisy[asked_flat].reshape(count, slots, width)
    fetched = lax.all_to_all(served, "space", split_axis=0, concat_axis=0, tiled=True)
    members = fetched.reshape(count * slots, width)[place].reshape(refs, group, width)
    coeffs = forward(members, cube_table, group_table)
    part, wcopy = first_phase(coeffs, sigma_coef, cube_table, group_table)
    buffer, wbuffer = pack_slots(part, wcopy, place, count, slots)
    returned, rweights = (
        lax.all_to_all(buffer, "space", split_axis=0, concat_axis=0, tiled=True),
        lax.all_to_all(wbuffer, "space", split_axis=0, concat_axis=0, tiled=True),
    )
    basic = aggregate(
        returned.reshape(-1, width), rweights.reshape(-1), asked_flat, noisy, rows_here
    )
    held_spectra = cube_spectra(basic, cube_table)
    served_spectra = held_spectra[asked_flat].reshape(count, slots, width)
    spectra_back = lax.all_to_all(
        served_spectra.astype(jnp.bfloat16), "space", split_axis=0, concat_axis=0, tiled=True
    ).astype(served_spectra.dtype)
    guide_spec = spectra_back.reshape(count * slots, width)[place].reshape(refs, group, width)
    gcoeffs = group_mix(guide_spec, group_table)
    part2, wcopy2 = second_phase(coeffs, gcoeffs, sigma_coef, cube_table, group_table)
    buffer2, wbuffer2 = pack_slots(part2, wcopy2, place, count, slots)
    returned2, rweights2 = (
        lax.all_to_all(buffer2, "space", split_axis=0, concat_axis=0, tiled=True),
        lax.all_to_all(wbuffer2, "space", split_axis=0, concat_axis=0, tiled=True),
    )
    final = aggregate(
        returned2.reshape(-1, width), rweights2.reshape(-1), asked_flat, noisy, rows_here
    )
    return (basic, final)


def solution(mesh):
    in_specs = (P(("groups", "space"), None), P(("groups", "space"), None), P("groups"), P())
    out_specs = (P(("groups", "space"), None), P(("groups", "space"), None))
    return jax.shard_map(body, mesh=mesh, in_specs=in_specs, out_specs=out_specs, check_vma=False)
```

profile of v0, /device:TPU:15, one launch (start us, length us, event | category | flops | bytes accessed | tf_op | source)
XLA Modules:
  0.0 499.9 jit_solution(1391775391187178127)
XLA Ops:
  0.6 0.8 copy.7
  1.6 8.4 %gather_fusion = s32[1536]{0:T(1024)S(1)} fusion(s32[8192]{0:T(1024)S(1)} %copy-done, s32[2048]{0:T(1024)S(1)} %pad_clamp_fusion.1), kind=kCustom, calls=%fused_computation | custom fusion | bytes 18432 | tf_op jit(solution)/shard_map/gather | solution.py:96
  10.1 4.5 reduce-window.6
  14.6 0.4 slice_reduce_fusion
  15.0 0.2 reduce-window.9
  15.2 0.1 add_add_fusion
  15.4 6.2 %scatter_custom_fusion = s32[3072]{0:T(1024)S(1)} fusion(s32[1536]{0:T(1024)S(1)} %fusion.29, s32[1536]{0:T(1024)S(1)} %get-tuple-element.6, s32[]{:T(128)} %constant.29.clone.1), kind=kCustom, calls=%fused_computation.88 | custom fusion | bytes 12292 | tf_op jit(solution)/shard_map/scatter | solution.py:103
  21.7 10.5 %all_to_all.49 = s32[16,1,192]{2,1,0:T(1,128)S(1)} all-to-all(s32[16,1,192]{2,1,0:T(1,128)S(1)} %all_to_all.30), channel_id=1, replica_groups=mesh['groups'=2,'space'=16] {'space'}, dimensions={0} | all-to-all | bytes 24576 | tf_op jit(solution)/shard_map/all_to_all | solution.py:104
  32.3 13.2 %gather_fusion.1 = bf16[3072,512]{1,0:T(8,128)(2,1)} fusion(bf16[512,512]{1,0:T(8,128)(2,1)S(1)} %copy-done.1, s32[3072]{0:T(1024)S(1)} %broadcast_clamp_fusion), kind=kCustom, calls=%fused_computation.1 | custom fusion | bytes 6303744 | tf_op jit(solution)/shard_map/gather | solution.py:106
  45.6 7.2 %all-to-all-start.1 = ((bf16[16,192,512]{2,1,0:T(8,128)(2,1)}), bf16[16,192,512]{2,1,0:T(8,128)(2,1)}, u32[]{:S(2)}, u32[]{:S(2)}) async-start(bf16[16,192,512]{2,1,0:T(8,128)(2,1)} %bitcast.109), calls=%async_computation.1 | async-start | bytes 6291456 | tf_op jit(solution)/shard_map/all_to_all | solution.py:107
  52.9 5.5 %fusion = bf16[8,8,8,8,8,8]{5,4,3,2,1,0:T(8,128)(2,1)} fusion(f32[8,8]{1,0:T(8,128)S(1)} %multiply_select_fusion.5, f32[8,8,8,8]{1,3,0,2:T(8,128)S(1)} %broadcast_multiply_fusion), kind=kLoop, calls=%fused_computation.15 | loop fusion | flops 524288 | bytes 540928 | tf_op jit(solution)/shard_map/convert_element_type | solution.py:22
  58.4 12.9 %reshape.414 = bf16[512,512,1]{1,0,2:T(8,128)(2,1)S(1)} reshape(bf16[8,8,8,8,8,8]{5,4,3,2,1,0:T(8,128)(2,1)} %fusion) | data formatting | bytes 1048576 | tf_op jit(solution)/shard_map/convert_element_type | solution.py:22
  71.4 51.2 %all-to-all-done.1 = bf16[16,192,512]{2,1,0:T(8,128)(2,1)} async-done(((bf16[16,192,512]{2,1,0:T(8,128)(2,1)}), bf16[16,192,512]{2,1,0:T(8,128)(2,1)}, u32[]{:S(2)}, u32[]{:S(2)}) %all-to-all-start.1) | async-done | bytes 3145760 | tf_op jit(solution)/shard_map/all_to_all | solution.py:107
  122.6 7.2 %gather_fusion.2 = bf16[1536,512]{1,0:T(8,128)(2,1)S(1)} fusion(bf16[3072,512]{1,0:T(8,128)(2,1)} %bitcast.4, s32[2048]{0:T(1024)S(1)} %pad_clamp_fusion), kind=kCustom, calls=%fused_computation.2 | custom fusion | bytes 3151872 | tf_op jit(solution)/shard_map/gather | solution.py:108
  129.8 1.0 fusion.75
  130.8 5.5 %multiply_reduce_fusion.1 = (f32[96]{0:T(128)S(1)}, f32[96,512,16]{1,2,0:T(8,128)}) fusion(f32[512]{0:T(512)S(1)} %get-tuple-element.8, f32[96,16,512]{2,1,0:T(8,128)S(1)} %fusion.75, f32[16]{0:T(128)S(1)} %add_multiply_fusion, pred[16]{0:T(512)(128)(4,1)S(1)} %iota_compare_fusion.2), kind=kOutput, calls=%fused_computation.30 | convolution fusion | flops 154928288 | bytes 6293968 | tf_op jit(solution)/shard_map/jm,rmk->rjk/dot_general | solution.py:32
  136.4 0.1 reshape.366
  136.5 11.6 %scatter_custom_fusion.3 = bf16[3072]{0:T(1024)(128)(2,1)S(1)} fusion(s32[1536]{0:T(1024)S(1)} %fusion.29, bf16[1536]{0:T(1024)(128)(2,1)S(1)} %reshape.366, bf16[]{:T(256)} %constant.40.clone.1), kind=kCustom, calls=%fused_computation.114 | custom fusion | bytes 6146 | tf_op jit(solution)/shard_map/scatter | solution.py:84
  148.1 0.7 all_to_all.40
  148.8 4.7 all-to-all-start.3
  153.6 5.4 %fusion.8 = bf16[96,512,16]{1,2,0:T(8,128)(2,1)S(1)} fusion(f32[96,512,16]{1,2,0:T(8,128)} %get-tuple-element.11, f32[512]{0:T(512)S(1)} %get-tuple-element.8, f32[16]{0:T(128)S(1)} %add_multiply_fusion, pred[16]{0:T(512)(128)(4,1)S(1)} %iota_compare_fusion.2), kind=kOutput, calls=%fused_computation.32 | convolution fusion | flops 154928384 | bytes 4720720 | tf_op jit(solution)/shard_map/jm,rjk->rmk/dot_general | solution.py:41
  159.0 1.0 multiply_convert_fusion.2
  160.0 9.6 %scatter_custom_fusion.1 = bf16[3072,512]{1,0:T(8,128)(2,1)} fusion(s32[1536]{0:T(1024)S(1)} %fusion.29, bf16[1536,512]{1,0:T(8,128)(2,1)S(1)} %bitcast.117, bf16[]{:T(256)} %constant.40.clone.1), kind=kCustom, calls=%fused_computation.38 | custom fusion | bytes 3145730 | tf_op jit(solution)/shard_map/scatter | solution.py:82
  169.5 6.0 %all-to-all-start.2 = ((bf16[16,192,512]{2,1,0:T(8,128)(2,1)}), bf16[16,192,512]{2,1,0:T(8,128)(2,1)}, u32[]{:S(2)}, u32[]{:S(2)}) async-start(bf16[16,192,512]{2,1,0:T(8,128)(2,1)} %bitcast.107), calls=%async_computation.2 | async-start | bytes 6291456 | tf_op jit(solution)/shard_map/all_to_all | solution.py:113
  175.6 12.9 %convert_element_type.89 = bf16[512,512]{1,0:T(8,128)(2,1)S(1)} reshape(bf16[8,8,8,8,8,8]{5,4,3,2,1,0:T(8,128)(2,1)} %fusion) | data formatting | bytes 1048576 | tf_op jit(solution)/shard_map/convert_element_type | solution.py:22
  188.4 0.1 convert_multiply_fusion
  188.6 1.0 copy.19
  189.8 21.7 %scatter_custom_fusion.4 = f32[512]{0:T(512)S(1)} fusion(s32[3072]{0:T(1024)S(1)} %reshape.356, f32[3072]{0:T(1024)S(1)} %reshape.374, f32[]{:T(128)} %constant.28.clone.1), kind=kCustom, calls=%fused_computation.119 | custom fusion | flops 3072 | bytes 2052 | tf_op jit(solution)/shard_map/scatter-add | solution.py:50
  211.5 34.0 %all-to-all-done.2 = bf16[16,192,512]{2,1,0:T(8,128)(2,1)} async-done(((bf16[16,192,512]{2,1,0:T(8,128)(2,1)}), bf16[16,192,512]{2,1,0:T(8,128)(2,1)}, u32[]{:S(2)}, u32[]{:S(2)}) %all-to-all-start.2) | async-done | bytes 3145760 | tf_op jit(solution)/shard_map/all_to_all | solution.py:113
  245.6 21.3 %scatter_custom_fusion.2 = f32[512,512]{1,0:T(8,128)S(1)} fusion(f32[512,512]{1,0:T(8,128)S(1)} %convert_multiply_fusion, s32[3072]{0:T(1024)S(1)} %reshape.356, bf16[3072,512]{1,0:T(8,128)(2,1)} %bitcast.23), kind=kCustom, calls=%fused_computation.18 | custom fusion | flops 3145728 | bytes 4194304 | tf_op jit(solution)/shard_map/scatter-add | solution.py:49
  266.9 0.1 divide_convert_fusion.1
  267.0 0.8 copy-done.5
  267.8 0.5 fusion.76
  268.3 13.2 %gather_fusion.3 = bf16[3072,512]{1,0:T(8,128)(2,1)} fusion(bf16[512,512]{1,0:T(8,128)(2,1)S(1)} %fusion.76, s32[3072]{0:T(1024)S(1)} %broadcast_clamp_fusion), kind=kCustom, calls=%fused_computation.3 | custom fusion | bytes 6303744 | tf_op jit(solution)/shard_map/gather | solution.py:120
  281.5 74.8 %all_to_all.50 = bf16[16,192,512]{2,1,0:T(8,128)(2,1)S(1)} all-to-all(bf16[16,192,512]{2,1,0:T(8,128)(2,1)} %bitcast.110), channel_id=1, replica_groups=mesh['groups'=2,'space'=16] {'space'}, dimensions={0} | all-to-all | bytes 6291456 | tf_op jit(solution)/shard_map/all_to_all | solution.py:121
  356.2 5.4 %gather_fusion.4 = bf16[1536,512]{1,0:T(8,128)(2,1)} fusion(bf16[3072,512]{1,0:T(8,128)(2,1)S(1)} %bitcast.106, s32[2048]{0:T(1024)S(1)} %pad_clamp_fusion), kind=kCustom, calls=%fused_computation.4 | custom fusion | bytes 3151872 | tf_op jit(solution)/shard_map/gather | solution.py:124
  361.7 4.7 multiply_reduce_fusion
  366.4 3.2 fusion.7
  369.7 11.1 %scatter_custom_fusion.7 = bf16[3072]{0:T(1024)(128)(2,1)S(1)} fusion(s32[1536]{0:T(1024)S(1)} %fusion.29, bf16[1536]{0:T(1024)(128)(2,1)S(1)} %reshape.398, bf16[]{:T(256)} %constant.40.clone.1), kind=kCustom, calls=%fused_computation.112 | custom fusion | bytes 6146 | tf_op jit(solution)/shard_map/scatter | solution.py:84
  380.8 0.7 all_to_all.41
  381.5 5.4 %all-to-all-start.6 = ((bf16[16,1,192]{2,1,0:T(2,128)(2,1)}), bf16[16,1,192]{2,1,0:T(2,128)(2,1)S(1)}, u32[]{:S(2)}, u32[]{:S(2)}) async-start(bf16[16,1,192]{2,1,0:T(2,128)(2,1)} %all_to_all.41), calls=%async_computation.6 | async-start | bytes 32768 | tf_op jit(solution)/shard_map/all_to_all | solution.py:130
  387.0 2.1 multiply_convert_fusion.1
  389.1 9.9 %scatter_custom_fusion.5 = bf16[3072,512]{1,0:T(8,128)(2,1)} fusion(s32[1536]{0:T(1024)S(1)} %fusion.29, bf16[1536,512]{1,0:T(8,128)(2,1)} %bitcast.116, bf16[]{:T(256)} %constant.40.clone.1), kind=kCustom, calls=%fused_computation.36 | custom fusion | bytes 3146240 | tf_op jit(solution)/shard_map/scatter | solution.py:82
  399.0 6.0 %all-to-all-start.5 = ((bf16[16,192,512]{2,1,0:T(8,128)(2,1)}), bf16[16,192,512]{2,1,0:T(8,128)(2,1)S(1)}, u32[]{:S(2)}, u32[]{:S(2)}) async-start(bf16[16,192,512]{2,1,0:T(8,128)(2,1)} %bitcast.21), calls=%async_computation.5 | async-start | bytes 6291456 | tf_op jit(solution)/shard_map/all_to_all | solution.py:129
  405.1 21.7 %scatter_custom_fusion.8 = f32[512]{0:T(512)S(1)} fusion(s32[3072]{0:T(1024)S(1)} %reshape.356, f32[3072]{0:T(1024)S(1)} %reshape.406, f32[]{:T(128)} %constant.28.clone.1), kind=kCustom, calls=%fused_computation.117 | custom fusion | flops 3072 | bytes 2052 | tf_op jit(solution)/shard_map/scatter-add | solution.py:50
  426.8 48.0 %all-to-all-done.5 = bf16[16,192,512]{2,1,0:T(8,128)(2,1)S(1)} async-done(((bf16[16,192,512]{2,1,0:T(8,128)(2,1)}), bf16[16,192,512]{2,1,0:T(8,128)(2,1)S(1)}, u32[]{:S(2)}, u32[]{:S(2)}) %all-to-all-start.5) | async-done | bytes 3145760 | tf_op jit(solution)/shard_map/all_to_all | solution.py:129
  474.9 22.6 %scatter_custom_fusion.6 = f32[512,512]{1,0:T(8,128)} fusion(f32[512,512]{1,0:T(8,128)} %copy.19, s32[3072]{0:T(1024)S(1)} %reshape.356, bf16[3072,512]{1,0:T(8,128)(2,1)S(1)} %bitcast.108), kind=kCustom, calls=%fused_computation.16 | custom fusion | flops 3145728 | bytes 4194304 | tf_op jit(solution)/shard_map/scatter-add | solution.py:49
  497.5 2.2 divide_convert_fusion
  (46 shorter events, 1.3 us)
Async XLA Ops:
  0.6 1.0 copy-start
  1.6 30.8 %copy-start.1 = (bf16[512,512]{1,0:T(8,128)(2,1)S(1)}, bf16[512,512]{1,0:T(8,128)(2,1)}, u32[]{:S(2)}) copy-start(bf16[512,512]{1,0:T(8,128)(2,1)} %param.4) | copy-start | bytes 1572868
  45.6 77.0 %all-to-all-start.1 = ((bf16[16,192,512]{2,1,0:T(8,128)(2,1)}), bf16[16,192,512]{2,1,0:T(8,128)(2,1)}, u32[]{:S(2)}, u32[]{:S(2)}) async-start(bf16[16,192,512]{2,1,0:T(8,128)(2,1)} %bitcast.109), calls=%async_computation.1 | async-start | bytes 6291456 | tf_op jit(solution)/shard_map/all_to_all | solution.py:107
  58.4 13.0 %copy-start.6 = (f32[512]{0:T(512)S(1)}, f32[512]{0:T(512)}, u32[]{:S(2)}) copy-start(f32[512]{0:T(512)} %param.7) | copy-start | bytes 6148
  71.3 87.7 %copy-start.3 = (bf16[512,512,1]{1,0,2:T(8,128)(2,1)}, bf16[512,512,1]{1,0,2:T(8,128)(2,1)S(1)}, u32[]{:S(2)}) copy-start(bf16[512,512,1]{1,0,2:T(8,128)(2,1)S(1)} %reshape.414) | copy-start | bytes 1572868
  148.8 20.7 %all-to-all-start.3 = ((bf16[16,1,192]{2,1,0:T(2,128)(2,1)}), bf16[16,1,192]{2,1,0:T(2,128)(2,1)S(1)}, u32[]{:S(2)}, u32[]{:S(2)}) async-start(bf16[16,1,192]{2,1,0:T(2,128)(2,1)} %all_to_all.40), calls=%async_computation.3 | async-start | bytes 32768 | tf_op jit(solution)/shard_map/all_to_all | solution.py:114
  169.5 76.0 %all-to-all-start.2 = ((bf16[16,192,512]{2,1,0:T(8,128)(2,1)}), bf16[16,192,512]{2,1,0:T(8,128)(2,1)}, u32[]{:S(2)}, u32[]{:S(2)}) async-start(bf16[16,192,512]{2,1,0:T(8,128)(2,1)} %bitcast.107), calls=%async_computation.2 | async-start | bytes 6291456 | tf_op jit(solution)/shard_map/all_to_all | solution.py:113
  267.0 0.8 copy-start.5
  361.7 4.7 copy-start.2
  366.4 20.6 %copy-start.4 = (bf16[512,512,1]{1,0,2:T(8,128)(2,1)S(1)}, bf16[512,512,1]{1,0,2:T(8,128)(2,1)}, u32[]{:S(2)}) copy-start(bf16[512,512,1]{1,0,2:T(8,128)(2,1)} %copy-done.3) | copy-start | bytes 1572868
  381.5 17.5 %all-to-all-start.6 = ((bf16[16,1,192]{2,1,0:T(2,128)(2,1)}), bf16[16,1,192]{2,1,0:T(2,128)(2,1)S(1)}, u32[]{:S(2)}, u32[]{:S(2)}) async-start(bf16[16,1,192]{2,1,0:T(2,128)(2,1)} %all_to_all.41), calls=%async_computation.6 | async-start | bytes 32768 | tf_op jit(solution)/shard_map/all_to_all | solution.py:130
  399.0 75.9 %all-to-all-start.5 = ((bf16[16,192,512]{2,1,0:T(8,128)(2,1)}), bf16[16,192,512]{2,1,0:T(8,128)(2,1)S(1)}, u32[]{:S(2)}, u32[]{:S(2)}) async-start(bf16[16,192,512]{2,1,0:T(8,128)(2,1)} %bitcast.21), calls=%async_computation.5 | async-start | bytes 6291456 | tf_op jit(solution)/shard_map/all_to_all | solution.py:129
where the time goes:
time: 504 us; the launch traced here: 500 us
  waiting for transfers between devices  133 us (26%)
  local copies, waits for them, and re-layouts  127 us (25%)
  other arithmetic  101 us (20%)
  blocking collectives  85.2 us (17%)
  starting transfers between devices  29.4 us (6%)
  matrix products  23.4 us (5%)
    all_to_all x1, blocking collectives, body(): lax.all_to_all(served_spectra.astype(jnp.bfloat16), 'space', split_axis=0...  74.8 us
    all_to_all x1, waiting for transfers between devices, body(): lax.all_to_all(served, 'space', split_axis=0, concat_axis=0, tiled=True)  51.2 us
    all_to_all x1, waiting for transfers between devices, body(): lax.all_to_all(buffer2, 'space', split_axis=0, concat_axis=0, tiled=True)  48 us
    scatter-add x2, other arithmetic, aggregate(): numer = jax.ops.segment_sum(parts.astype(jnp.float32), targets, count)  43.9 us
    scatter-add x2, other arithmetic, aggregate(): denom = jax.ops.segment_sum(weights.astype(jnp.float32), targets, count)  43.4 us
    all_to_all x1, waiting for transfers between devices, body(): lax.all_to_all(buffer, 'space', split_axis=0, concat_axis=0, tiled=True)  34 us
    convert_element_type x2, local copies, waits for them, and re-layouts, make_tables(): jnp.einsum('ad,be,cf->abcdef', small, small, small).reshape(512, 512)  25.8 us
    scatter x2, local copies, waits for them, and re-layouts, pack_slots(): jnp.zeros((count * slots,), jnp.bfloat16).at[place]  22.7 us
  transfers between devices with their start and end apart: 5, of which 3 were waited for; matrix products, arithmetic and copies ran while one was open for 21% of the time, Pallas kernels for 0%

commit v1 on v0

v1 whole, which is shorter than its diff:
```python
import functools

import jax
import jax.numpy as jnp
import numpy as np
from jax import lax
from jax.experimental import pallas as pl
from jax.experimental.pallas import tpu as pltpu
from jax.sharding import PartitionSpec as P

shrink_level = 2.7
prior_weight = 0.5
LANES = 128
CHUNK = 512
ROWS = 256


def dct_matrix(length):
    index = np.arange(length, dtype=np.float64)
    table = np.cos(np.pi * (2.0 * index[None, :] + 1.0) * index[:, None] / (2.0 * length))
    table = table * np.sqrt(2.0 / length)
    table[0] /= np.sqrt(2.0)
    return table


def make_tables(group):
    small = dct_matrix(8)
    cube = np.kron(np.kron(small, small), small).astype(np.float32)
    mix = np.kron(np.eye(LANES // group), dct_matrix(group)).astype(np.float32)
    return jnp.asarray(cube, jnp.bfloat16), jnp.asarray(cube.T, jnp.bfloat16), mix, mix.T.copy()


def mix_rows(table, value):
    pieces = [
        jnp.dot(
            table,
            value[i : i + LANES],
            precision=lax.Precision.HIGHEST,
            preferred_element_type=jnp.float32,
        )
        for i in range(0, value.shape[0], LANES)
    ]
    return jnp.concatenate(pieces, axis=0)


def kernel(second, group, *refs):
    if second:
        (home, ids, sigma, cube, cube_t, mix, mix_t, coeffs, table, acc_out, wsum) = refs[:11]
        big, members, wacc, wref, stage, sem = refs[11:]
    else:
        (home, ids, sigma, cube, cube_t, mix, mix_t, table, coeffs, acc_out, wsum) = refs[:11]
        big, members, wacc, wref, stage, sem = refs[11:]
    cubes, width = table.shape
    entries = members.shape[0]
    chunks = cubes // CHUNK

    def fetch(i, slot):
        rows = pl.ds(pl.multiple_of(i * CHUNK, CHUNK), CHUNK)
        return pltpu.make_async_copy(table.at[rows, :], stage.at[slot], sem.at[slot])

    fetch(0, 0).start()

    def load_step(i, carry):
        slot = lax.rem(i, 2)

        @pl.when(i + 1 < chunks)
        def _():
            fetch(i + 1, 1 - slot).start()

        fetch(i, slot).wait()
        rows = pl.ds(pl.multiple_of(i * CHUNK, CHUNK), CHUNK)
        big[rows, :] = stage[slot].astype(jnp.float32)
        return carry

    lax.fori_loop(0, chunks, load_step, 0)

    def gather_step(r, carry):
        base = pl.multiple_of(r * group, group)
        picked = [big[pl.ds(home[ids[base + m]], 1), :] for m in range(group)]
        for m in range(group):
            members[pl.ds(base + m, 1), :] = picked[m]
        return carry

    lax.fori_loop(0, entries // group, gather_step, 0)

    noise = sigma[...] * sigma[...]
    level = (shrink_level * sigma[...]) * (shrink_level * sigma[...])

    def compute_step(b, carry):
        rows = pl.ds(pl.multiple_of(b * ROWS, ROWS), ROWS)
        spec = jnp.dot(
            members[rows, :].astype(jnp.bfloat16), cube_t[...], preferred_element_type=jnp.float32
        )
        own = mix_rows(mix[...], spec)
        square = own * own
        if second:
            gain = square / (square + noise)
            energy = gain * gain * noise
            shrunk = gain * coeffs[rows, :]
        else:
            coeffs[rows, :] = own
            gain = square / (square + level)
            energy = gain * gain
            shrunk = gain * own
        refs_here = ROWS // group
        total = jnp.sum(jnp.sum(energy, axis=1, keepdims=True).reshape(refs_here, group, 1), axis=1)
        weight = 1.0 / (0.25 + total / (group * width))
        back = mix_rows(mix_t[...], shrunk).astype(jnp.bfloat16)
        out = jnp.dot(back, cube[...], preferred_element_type=jnp.float32)
        each = jnp.broadcast_to(weight[:, None, :], (refs_here, group, 1)).reshape(ROWS, 1)
        members[rows, :] = (each * out).astype(jnp.bfloat16).astype(jnp.float32)
        wref[pl.ds(pl.multiple_of(b * refs_here, refs_here), refs_here), :] = jnp.broadcast_to(
            weight.astype(jnp.bfloat16).astype(jnp.float32), (refs_here, LANES)
        )
        return carry

    lax.fori_loop(0, entries // ROWS, compute_step, 0)

    def zero_step(i, carry):
        rows = pl.ds(pl.multiple_of(i * CHUNK, CHUNK), CHUNK)
        big[rows, :] = jnp.zeros((CHUNK, width), jnp.float32)
        wacc[rows, :] = jnp.zeros((CHUNK, LANES), jnp.float32)
        return carry

    lax.fori_loop(0, chunks, zero_step, 0)

    def scatter_step(r, carry):
        base = pl.multiple_of(r * group, group)
        wrow = wref[pl.ds(r, 1), :]
        for m in range(group):
            row = pl.ds(home[ids[base + m]], 1)
            big[row, :] += members[pl.ds(base + m, 1), :]
            wacc[row, :] += wrow
        return carry

    lax.fori_loop(0, entries // group, scatter_step, 0)

    def put(i, slot):
        rows = pl.ds(pl.multiple_of(i * CHUNK, CHUNK), CHUNK)
        return pltpu.make_async_copy(stage.at[slot], acc_out.at[rows, :], sem.at[slot])

    def store_step(i, carry):
        slot = lax.rem(i, 2)

        @pl.when(i >= 2)
        def _():
            put(i - 2, slot).wait()

        rows = pl.ds(pl.multiple_of(i * CHUNK, CHUNK), CHUNK)
        stage[slot] = big[rows, :].astype(jnp.bfloat16)
        put(i, slot).start()
        return carry

    lax.fori_loop(0, chunks, store_step, 0)

    lane = lax.broadcasted_iota(jnp.int32, (LANES, LANES), 1)
    sub = lax.broadcasted_iota(jnp.int32, (LANES, LANES), 0)

    def weight_step(i, carry):
        rows = pl.ds(pl.multiple_of(i * LANES, LANES), LANES)
        wsum[pl.ds(i, 1), :] = jnp.sum(
            jnp.where(lane == sub, wacc[rows, :], 0.0), axis=0, keepdims=True
        )
        return carry

    lax.fori_loop(0, cubes // LANES, weight_step, 0)
    for i in (chunks - 2, chunks - 1):
        put(i, i % 2).wait()


def phase(second, home, ids, sigma, tables, table, group, coeffs=None):
    cubes, width = table.shape
    entries = ids.shape[0]
    vmem = pl.BlockSpec(memory_space=pltpu.VMEM)
    smem = pl.BlockSpec(memory_space=pltpu.SMEM)
    anywhere = pl.BlockSpec(memory_space=pltpu.HBM)
    held = jax.ShapeDtypeStruct((entries, width), jnp.float32)
    outs = [
        jax.ShapeDtypeStruct((cubes, width), jnp.bfloat16),
        jax.ShapeDtypeStruct((cubes // LANES, LANES), jnp.float32),
    ]
    out_specs = [anywhere, vmem]
    in_specs = [smem, smem] + [vmem] * 5
    args = [home, ids, sigma, *tables]
    if second:
        in_specs = in_specs + [vmem, anywhere]
        args = args + [coeffs, table]
    else:
        in_specs = in_specs + [anywhere]
        args = args + [table]
        outs = [held] + outs
        out_specs = [vmem] + out_specs
    return pl.pallas_call(
        functools.partial(kernel, second, group),
        out_shape=outs,
        in_specs=in_specs,
        out_specs=out_specs,
        scratch_shapes=[
            pltpu.VMEM((cubes, width), jnp.float32),
            pltpu.VMEM((entries, width), jnp.float32),
            pltpu.VMEM((cubes, LANES), jnp.float32),
            pltpu.VMEM((entries // group, LANES), jnp.float32),
            pltpu.VMEM((2, CHUNK, width), jnp.bfloat16),
            pltpu.SemaphoreType.DMA((2,)),
        ],
        compiler_params=pltpu.CompilerParams(vmem_limit_bytes=60 * 1024 * 1024),
        name="wiener" if second else "shrink",
    )(*args)


MESH = pl.DeviceIdType.MESH


class Ring:
    def __init__(self, grid, count):
        self.grid, self.chips = grid, count // 2
        self.me = lax.axis_index("space")
        self.core = lax.rem(self.me, 2)
        self.spot = self.spot_of(self.me // 2)
        self.partner = {"space": self.me + 1 - 2 * self.core}
        self.sides = tuple({"space": self.device(sign, self.core)} for sign in (1, -1))

    def spot_of(self, chip):
        if self.grid == 1:
            return chip
        side, along = lax.rem(chip, 2), chip // 2
        return along + side * (self.chips - 1 - 2 * along)

    def chip(self, offset):
        spot = lax.rem(self.spot + offset + self.chips, self.chips)
        if self.grid == 1:
            return spot
        side = (2 * spot) // self.chips
        return (spot + side * (self.chips - 1 - 2 * spot)) * 2 + side

    def device(self, offset, core):
        return self.chip(offset) * 2 + core

    def greet(self):
        barrier = pltpu.get_barrier_semaphore()
        for device in (*self.sides, self.partner):
            pl.semaphore_signal(barrier, inc=1, device_id=device, device_id_type=MESH)
        pl.semaphore_wait(barrier, 3)


def hops(chips, pieces):
    far = chips // 2
    orders = []
    for way in range(2):
        halves = range(pieces // 2) if way == 0 else range(pieces // 2, pieces)
        orders.append([(d, j) for d in range(1, far) for j in range(pieces)] + [(far, j) for j in halves])
    return orders


def remote(src, dst, send, recv, device):
    return pltpu.make_async_remote_copy(
        src_ref=src, dst_ref=dst, send_sem=send, recv_sem=recv, device_id=device, device_id_type=MESH
    )


def gather_kernel(grid, x, out, send, recv, give, take, own):
    count, held = out.shape[:2]
    pieces = held // LANES
    ring = Ring(grid, count)
    orders = hops(ring.chips, pieces)
    where = [{key: t for t, key in enumerate(order)} for order in orders]
    last = len(orders[0])
    ring.greet()

    def part(block, j):
        return out.at[block, pl.ds(j * LANES, LANES), :]

    started = []

    def start(copy):
        copy.start()
        started.append(copy)

    for j in range(pieces):
        for way in range(2):
            if (1, j) in where[way]:
                t = where[way][(1, j)]
                start(
                    remote(
                        x.at[pl.ds(j * LANES, LANES), :],
                        part(ring.me, j),
                        send.at[way, t],
                        recv.at[way, t],
                        ring.sides[way],
                    )
                )
    keep = pltpu.make_async_copy(x, out.at[ring.me], own.at[0])
    keep.start()
    start(remote(x, out.at[ring.me], give.at[0, last], take.at[0, last], ring.partner))
    for t in range(last):
        for way in range(2):
            d, j = orders[way][t]
            block = ring.device(-d if way == 0 else d, ring.core)
            piece = part(block, j)
            remote(piece, piece, send.at[way, t], recv.at[way, t], ring.sides[way]).wait_recv()
            onward = where[way].get((d + 1, j))
            if onward is not None:
                start(
                    remote(
                        piece, piece, send.at[way, onward], recv.at[way, onward], ring.sides[way]
                    )
                )
            start(remote(piece, piece, give.at[way, t], take.at[way, t], ring.partner))
    other = ring.me + 1 - 2 * ring.core
    remote(
        out.at[other], out.at[other], give.at[0, last], take.at[0, last], ring.partner
    ).wait_recv()
    for t in range(last):
        for way in range(2):
            d, j = orders[way][t]
            piece = part(ring.device(-d if way == 0 else d, 1 - ring.core), j)
            remote(piece, piece, give.at[way, t], take.at[way, t], ring.partner).wait_recv()
    for copy in started:
        copy.wait_send()
    keep.wait()


def gather_all(x, grid):
    count = lax.axis_size("space")
    held, width = x.shape
    last = len(hops(count // 2, held // LANES)[0])
    sems = pltpu.SemaphoreType.DMA
    out = pl.pallas_call(
        functools.partial(gather_kernel, grid),
        out_shape=jax.ShapeDtypeStruct((count, held, width), x.dtype),
        in_specs=[pl.BlockSpec(memory_space=pltpu.VMEM)],
        out_specs=pl.BlockSpec(memory_space=pltpu.HBM),
        scratch_shapes=[
            sems((2, last)),
            sems((2, last)),
            sems((2, last + 1)),
            sems((2, last + 1)),
            sems((1,)),
        ],
        compiler_params=pltpu.CompilerParams(collective_id=0, has_side_effects=True),
        name="spread",
    )(x)
    return out.reshape(count * held, width)


def reduce_kernel(grid, acc, wsum, noisy, out, own, other, got, sent, wother, wgot, wsent, *sems):
    own_sem, give, take, send, recv, wgive, wtake, wsend, wrecv = sems
    chips = acc.shape[0]
    pieces = acc.shape[2] // LANES
    ring = Ring(grid, 2 * chips)
    far = chips // 2
    orders = [
        sorted(order, key=lambda key: (-key[0], key[1])) for order in hops(chips, pieces)
    ]
    where = [{key: t for t, key in enumerate(order)} for order in orders]
    last = len(orders[0])
    offsets = [far] + [s * d for d in range(far - 1, 0, -1) for s in (1, -1)] + [0]
    slot_of = {off: i for i, off in enumerate(offsets)}
    slot_of[-far] = 0
    started, local, gifts = [], [], []

    for i, off in enumerate(offsets):
        copy = pltpu.make_async_copy(acc.at[ring.chip(off), ring.core], own.at[i], own_sem.at[i])
        copy.start()
        local.append(copy)
    ring.greet()
    for i, off in enumerate(offsets):
        copy = remote(
            acc.at[ring.chip(off), 1 - ring.core], other.at[i], give.at[i], take.at[i], ring.partner
        )
        copy.start()
        gifts.append(copy)
        if i == 0:
            wgift = remote(wsum, wother, wgive.at[0], wtake.at[0], ring.partner)
            wgift.start()
    ready = set()

    def settle_slot(i):
        if i not in ready:
            ready.add(i)
            local[i].wait()
            gifts[i].wait_recv()

    def value(off, j, ways, d):
        i = slot_of[off]
        settle_slot(i)
        rows = pl.ds(j * LANES, LANES)
        total = own[i, rows, :].astype(jnp.float32) + other[i, rows, :].astype(jnp.float32)
        for way in ways:
            t = where[way].get((d + 1, j))
            if t is not None:
                piece = got.at[way, t]
                remote(sent.at[way, t], piece, send.at[way, t], recv.at[way, t], ring.sides[way]).wait_recv()
                total = total + piece[...].astype(jnp.float32)
        return total

    def weights(off, ways, d):
        chip = ring.chip(off)
        if "w" not in ready:
            ready.add("w")
            wgift.wait_recv()
        total = wsum[chip, ring.core] + wother[chip, ring.core]
        for way in ways:
            if d + 1 < far or (d + 1 == far and way == 0):
                remote(
                    wsent.at[way, d + 1],
                    wgot.at[way, d + 1],
                    wsend.at[way, d + 1],
                    wrecv.at[way, d + 1],
                    ring.sides[way],
                ).wait_recv()
                total = total + wgot[way, d + 1]
        return total

    for t in range(last):
        for way in range(2):
            d, j = orders[way][t]
            off = d if way == 0 else -d
            sent[way, t] = value(off, j, (way,), d).astype(sent.dtype)
            copy = remote(sent.at[way, t], got.at[way, t], send.at[way, t], recv.at[way, t], ring.sides[way])
            copy.start()
            started.append(copy)
            final_piece = t + 1 == last or orders[way][t + 1][0] != d
            if final_piece and (d < far or way == 0):
                wsent[way, d] = weights(off, (way,), d)
                copy = remote(
                    wsent.at[way, d], wgot.at[way, d], wsend.at[way, d], wrecv.at[way, d], ring.sides[way]
                )
                copy.start()
                started.append(copy)
    lane = lax.broadcasted_iota(jnp.int32, (LANES, LANES), 1)
    sub = lax.broadcasted_iota(jnp.int32, (LANES, LANES), 0)
    denom = weights(0, (0, 1), 0)
    for j in range(pieces):
        rows = pl.ds(j * LANES, LANES)
        numer = value(0, j, (0, 1), 0) + prior_weight * noisy[rows, :].astype(jnp.float32)
        spread = jnp.broadcast_to(denom[j : j + 1, :], (LANES, LANES))
        column = jnp.sum(jnp.where(lane == sub, spread, 0.0), axis=1, keepdims=True)
        out[rows, :] = (numer / (column + prior_weight)).astype(out.dtype)
    for copy in started + gifts + [wgift]:
        copy.wait_send()


def settle(acc, wsum, noisy, grid):
    count = lax.axis_size("space")
    held, width = noisy.shape
    chips, pieces = count // 2, held // LANES
    far = chips // 2
    last = len(hops(chips, pieces)[0])
    sems = pltpu.SemaphoreType.DMA
    vmem = pl.BlockSpec(memory_space=pltpu.VMEM)
    small = (chips, 2, pieces, LANES)
    return pl.pallas_call(
        functools.partial(reduce_kernel, grid),
        out_shape=jax.ShapeDtypeStruct(noisy.shape, noisy.dtype),
        in_specs=[pl.BlockSpec(memory_space=pltpu.HBM), vmem, vmem],
        out_specs=vmem,
        scratch_shapes=[
            pltpu.VMEM((chips, held, width), acc.dtype),
            pltpu.VMEM((chips, held, width), acc.dtype),
            pltpu.VMEM((2, last, LANES, width), acc.dtype),
            pltpu.VMEM((2, last, LANES, width), acc.dtype),
            pltpu.VMEM(small, jnp.float32),
            pltpu.VMEM((2, far + 1, pieces, LANES), jnp.float32),
            pltpu.VMEM((2, far + 1, pieces, LANES), jnp.float32),
            sems((chips,)),
            sems((chips,)),
            sems((chips,)),
            sems((2, last)),
            sems((2, last)),
            sems((1,)),
            sems((1,)),
            sems((2, far + 1)),
            sems((2, far + 1)),
        ],
        compiler_params=pltpu.CompilerParams(
            collective_id=1, has_side_effects=True, vmem_limit_bytes=60 * 1024 * 1024
        ),
        name="settle",
    )(acc.reshape(chips, 2, held, width), wsum.reshape(small), noisy)


def body(grid, noisy, matches, cube_home, sigma_coef):
    group = matches.shape[1]
    tables = make_tables(group)
    ids = matches.reshape(-1)
    sigma = sigma_coef[None, :]
    table = gather_all(noisy, grid)
    coeffs, acc, wsum = phase(False, cube_home, ids, sigma, tables, table, group)
    basic = settle(acc, wsum, noisy, grid)
    guide = gather_all(basic, grid)
    acc2, wsum2 = phase(True, cube_home, ids, sigma, tables, guide, group, coeffs)
    return basic, settle(acc2, wsum2, noisy, grid)


def solution(mesh):
    in_specs = (P(("groups", "space"), None), P(("groups", "space"), None), P("groups"), P())
    out_specs = (P(("groups", "space"), None), P(("groups", "space"), None))
    grid = 2 if mesh.shape["groups"] == 2 else 1
    return jax.shard_map(
        functools.partial(body, grid),
        mesh=mesh,
        in_specs=in_specs,
        out_specs=out_specs,
        check_vma=False,
    )
```

time: 504 us -> 285 us (0.57)
  Pallas kernels: 0 us -> 277 us
  waiting for transfers between devices: 133 us -> 0 us
  local copies, waits for them, and re-layouts: 127 us -> 4.14 us
  other arithmetic: 101 us -> 0 us
  blocking collectives: 85.2 us -> 0 us
  starting transfers between devices: 29.4 us -> 0 us
  matrix products: 23.4 us -> 0 us
    pallas_call x0 -> x6, Pallas kernels: none -> 277 us  [the longest x2 94.6 us: settle(): pl.pallas_call(functools.partial(reduce_kernel, grid), out_shape=jax.Shap...]
    all_to_all x5 -> x0, waiting for transfers between devices: 133 us -> none  [the longest x1 51.2 us: body(): lax.all_to_all(served, 'space', split_axis=0, concat_axis=0, tiled=True)]
    scatter-add x4 -> x0, other arithmetic: 87.3 us -> none  [the longest x2 43.9 us: aggregate(): numer = jax.ops.segment_sum(parts.astype(jnp.float32), targets, count)]
    all_to_all x2 -> x0, blocking collectives: 85.2 us -> none  [the longest x1 74.8 us: body(): lax.all_to_all(served_spectra.astype(jnp.bfloat16), 'space', split_axis=0...]
    scatter x5 -> x0, local copies, waits for them, and re-layouts: 48.3 us -> none  [the longest x2 22.7 us: pack_slots(): jnp.zeros((count * slots,), jnp.bfloat16).at[place]]
    gather x5 -> x0, local copies, waits for them, and re-layouts: 47.4 us -> none  [the longest x1 13.2 us: body(): served = noisy[asked_flat].reshape(count, slots, width)]
    all_to_all x5 -> x0, starting transfers between devices: 29.4 us -> none  [the longest x1 7.15 us: body(): lax.all_to_all(served, 'space', split_axis=0, concat_axis=0, tiled=True)]
    convert_element_type x4 -> x0, local copies, waits for them, and re-layouts: 25.9 us -> none  [the longest x2 25.8 us: make_tables(): jnp.einsum('ad,be,cf->abcdef', small, small, small).reshape(512, 512)]
  transfers between devices with their start and end apart: 5 -> 0, of which waited for: 3 -> 0; matrix products, arithmetic and copies ran while one was open for 21% -> 0% of each run, Pallas kernels for 0% -> 0%
where the time goes in v1:
time: 285 us; the launch traced here: 281 us
  Pallas kernels  277 us (97%)
  local copies, waits for them, and re-layouts  4.14 us (1%)
    pallas_call x2, Pallas kernels, settle(): pl.pallas_call(functools.partial(reduce_kernel, grid), out_shape=jax.Shap...  94.6 us
    pallas_call x2, Pallas kernels, gather_all(): pl.pallas_call(functools.partial(gather_kernel, grid), out_shape=jax.Shap...  93.3 us
    pallas_call x2, Pallas kernels, phase(): pl.pallas_call(functools.partial(kernel, second, group), out_shape=outs,...  88.6 us

profile of v1, /device:TPU:15, one launch (start us, length us, event | category | flops | bytes accessed | tf_op | source)
XLA Modules:
  0.0 281.3 jit_solution(8744619863726018855)
XLA Ops:
  0.6 0.8 copy.10
  1.4 0.7 reshape.25.refs_1_
  2.1 47.2 %spread.2 = bf16[16,512,512]{2,1,0:T(8,128)(2,1)} custom-call(bf16[512,512]{1,0:T(8,128)(2,1)} %noisy.3), custom_call_target="tpu_custom_call" | custom-call | tf_op jit(solution)/shard_map/spread/pallas_call | solution.py:328
  49.3 44.5 %shrink.1 = (f32[1536,512]{1,0:T(8,128)}, bf16[8192,512]{1,0:T(8,128)(2,1)}, f32[64,128]{1,0:T(8,128)}) custom-call(s32[8192]{0:T(1024)} %refs_0_.3, s32[1536]{0:T(1024)} %reshape.25.refs_1_, f32[1,512]{1,0:T(1,128)} %bitcast.13, bf16[512,512]{1,0:T(8,128)(2,1)} %constant.8.clone.refs_3_, bf16[512,512]{1,0:T(8,128)(2,1)} %constant.9.clone.refs_4_, ...), custom_call_target="tpu_custom_call" | custom-call | tf_op jit(solution)/shard_map/shrink/pallas_call | solution.py:193
  93.8 47.3 %settle.2.x = bf16[512,512]{1,0:T(8,128)(2,1)} custom-call(bf16[8,2,512,512]{3,2,1,0:T(8,128)(2,1)} %bitcast.10, f32[8,2,4,128]{3,2,1,0:T(4,128)} %bitcast.12, bf16[512,512]{1,0:T(8,128)(2,1)} %noisy.3), custom_call_target="tpu_custom_call" | custom-call | tf_op jit(solution)/shard_map/settle/pallas_call | solution.py:453
  141.1 46.1 %spread.3 = bf16[16,512,512]{2,1,0:T(8,128)(2,1)} custom-call(bf16[512,512]{1,0:T(8,128)(2,1)} %settle.2.x), custom_call_target="tpu_custom_call" | custom-call | tf_op jit(solution)/shard_map/spread/pallas_call | solution.py:328
  187.2 0.0 copy-start
  187.2 44.1 %wiener.1 = (bf16[8192,512]{1,0:T(8,128)(2,1)}, f32[64,128]{1,0:T(8,128)}) custom-call(s32[8192]{0:T(1024)} %refs_0_.3, s32[1536]{0:T(1024)} %reshape.25.refs_1_, f32[1,512]{1,0:T(1,128)} %bitcast.14, bf16[512,512]{1,0:T(8,128)(2,1)} %constant.8.clone.refs_3_, bf16[512,512]{1,0:T(8,128)(2,1)} %constant.9.clone.refs_4_, f32[128,128]{1,0:T(8,128)} %constant.10.clone.refs_5_, ...), custom_call_target="tpu_custom_call" | custom-call | tf_op jit(solution)/shard_map/wiener/pallas_call | solution.py:193
  231.3 47.3 %settle.3 = bf16[512,512]{1,0:T(8,128)(2,1)} custom-call(bf16[8,2,512,512]{3,2,1,0:T(8,128)(2,1)} %bitcast.9, f32[8,2,4,128]{3,2,1,0:T(4,128)} %bitcast.11, bf16[512,512]{1,0:T(8,128)(2,1)} %noisy.3), custom_call_target="tpu_custom_call" | custom-call | tf_op jit(solution)/shard_map/settle/pallas_call | solution.py:453
  278.7 0.0 copy-done
  278.7 0.8 copy.13
  279.5 1.9 copy.14
Async XLA Ops:
  187.2 91.4 %copy-start = (bf16[512,512]{1,0:T(8,128)(2,1)S(1)}, bf16[512,512]{1,0:T(8,128)(2,1)}, u32[]{:S(2)}) copy-start(bf16[512,512]{1,0:T(8,128)(2,1)} %settle.2.x) | copy-start | bytes 1572868

commit v2 on v1

--- a/solution.py
+++ b/solution.py
@@ -12,7 +12,8 @@
 prior_weight = 0.5
 LANES = 128
 CHUNK = 512
-ROWS = 256
+ROWS = 384
+TOGETHER = 2
 
 
 def dct_matrix(length):
@@ -23,36 +24,48 @@
     return table
 
 
+def split(value):
+    high = value.astype(jnp.bfloat16)
+    return high, (value - high.astype(jnp.float32)).astype(jnp.bfloat16)
+
+
 def make_tables(group):
     small = dct_matrix(8)
     cube = np.kron(np.kron(small, small), small).astype(np.float32)
     mix = np.kron(np.eye(LANES // group), dct_matrix(group)).astype(np.float32)
-    return jnp.asarray(cube, jnp.bfloat16), jnp.asarray(cube.T, jnp.bfloat16), mix, mix.T.copy()
+    mixes = [
+        np.concatenate([np.asarray(half, np.float32) for half in split(each)], axis=1)
+        for each in (mix, mix.T)
+    ]
+    return (cube.astype(jnp.bfloat16), cube.T.astype(jnp.bfloat16)) + tuple(
+        each.astype(jnp.bfloat16) for each in mixes
+    )
 
 
 def mix_rows(table, value):
-    pieces = [
-        jnp.dot(
-            table,
-            value[i : i + LANES],
-            precision=lax.Precision.HIGHEST,
-            preferred_element_type=jnp.float32,
+    both, high = table, table[:, :LANES]
+    pieces = []
+    for i in range(0, value.shape[0], LANES):
+        top, low = split(value[i : i + LANES])
+        pieces.append(
+            jnp.dot(both, jnp.concatenate([top, top], axis=0), preferred_element_type=jnp.float32)
+            + jnp.dot(high, low, preferred_element_type=jnp.float32)
         )
-        for i in range(0, value.shape[0], LANES)
-    ]
     return jnp.concatenate(pieces, axis=0)
 
 
 def kernel(second, group, *refs):
     if second:
-        (home, ids, sigma, cube, cube_t, mix, mix_t, coeffs, table, acc_out, wsum) = refs[:11]
-        big, members, wacc, wref, stage, sem = refs[11:]
+        (rows_in, sigma, cube, cube_t, mix, mix_t, coeffs, table, acc_out, wsum) = refs[:10]
     else:
-        (home, ids, sigma, cube, cube_t, mix, mix_t, table, coeffs, acc_out, wsum) = refs[:11]
-        big, members, wacc, wref, stage, sem = refs[11:]
+        (home, ids, sigma, cube, cube_t, mix, mix_t, table, coeffs, rows_in, acc_out, wsum) = refs[:12]
+    big, members, stage, sem = refs[-4:]
     cubes, width = table.shape
-    entries = members.shape[0]
+    full = big.shape[1]
+    groups = members.shape[0]
+    entries = groups * group
     chunks = cubes // CHUNK
+    steps = entries // ROWS
 
     def fetch(i, slot):
         rows = pl.ds(pl.multiple_of(i * CHUNK, CHUNK), CHUNK)
@@ -69,28 +82,37 @@
 
         fetch(i, slot).wait()
         rows = pl.ds(pl.multiple_of(i * CHUNK, CHUNK), CHUNK)
-        big[rows, :] = stage[slot].astype(jnp.float32)
+        big[rows, :width] = stage[slot].astype(jnp.float32)
         return carry
 
     lax.fori_loop(0, chunks, load_step, 0)
 
     def gather_step(r, carry):
-        base = pl.multiple_of(r * group, group)
-        picked = [big[pl.ds(home[ids[base + m]], 1), :] for m in range(group)]
+        base = r * group
+        places = [rows_in[base + m] if second else home[ids[base + m]] for m in range(group)]
+        if not second:
+            for m in range(group):
+                rows_in[base + m] = places[m]
+        picked = [big[pl.ds(places[m], 1), :] for m in range(group)]
         for m in range(group):
-            members[pl.ds(base + m, 1), :] = picked[m]
+            members[r, m : m + 1, :] = picked[m]
         return carry
 
-    lax.fori_loop(0, entries // group, gather_step, 0)
+    lax.fori_loop(0, groups, gather_step, 0)
 
     noise = sigma[...] * sigma[...]
     level = (shrink_level * sigma[...]) * (shrink_level * sigma[...])
 
     def compute_step(b, carry):
         rows = pl.ds(pl.multiple_of(b * ROWS, ROWS), ROWS)
-        spec = jnp.dot(
-            members[rows, :].astype(jnp.bfloat16), cube_t[...], preferred_element_type=jnp.float32
+        refs_here = ROWS // group
+        some = pl.ds(b * refs_here, refs_here)
+        taken = members[some, :, :width].reshape(ROWS, width).astype(jnp.bfloat16)
+        cleared = cubes // steps
+        big[pl.ds(pl.multiple_of(b * cleared, cleared), cleared), :] = jnp.zeros(
+            (cleared, full), jnp.float32
         )
+        spec = jnp.dot(taken, cube_t[...], preferred_element_type=jnp.float32)
         own = mix_rows(mix[...], spec)
         square = own * own
         if second:
@@ -102,38 +124,36 @@
             gain = square / (square + level)
             energy = gain * gain
             shrunk = gain * own
-        refs_here = ROWS // group
         total = jnp.sum(jnp.sum(energy, axis=1, keepdims=True).reshape(refs_here, group, 1), axis=1)
         weight = 1.0 / (0.25 + total / (group * width))
         back = mix_rows(mix_t[...], shrunk).astype(jnp.bfloat16)
         out = jnp.dot(back, cube[...], preferred_element_type=jnp.float32)
         each = jnp.broadcast_to(weight[:, None, :], (refs_here, group, 1)).reshape(ROWS, 1)
-        members[rows, :] = (each * out).astype(jnp.bfloat16).astype(jnp.float32)
-        wref[pl.ds(pl.multiple_of(b * refs_here, refs_here), refs_here), :] = jnp.broadcast_to(
-            weight.astype(jnp.bfloat16).astype(jnp.float32), (refs_here, LANES)
+        part = (each * out).astype(jnp.bfloat16).astype(jnp.float32)
+        members[some, :, :width] = part.reshape(refs_here, group, width)
+        members[some, :, width:] = jnp.broadcast_to(
+            weight[:, None, :].astype(jnp.bfloat16).astype(jnp.float32), (refs_here, group, LANES)
         )
         return carry
 
-    lax.fori_loop(0, entries // ROWS, compute_step, 0)
-
-    def zero_step(i, carry):
-        rows = pl.ds(pl.multiple_of(i * CHUNK, CHUNK), CHUNK)
-        big[rows, :] = jnp.zeros((CHUNK, width), jnp.float32)
-        wacc[rows, :] = jnp.zeros((CHUNK, LANES), jnp.float32)
+    lax.fori_loop(0, steps, compute_step, 0)
+
+    def scatter_step(r, carry):
+        base = r * group
+        for first in range(0, group, TOGETHER):
+            places = [rows_in[base + first + m] for m in range(TOGETHER)]
+            added = [members[r, first + m : first + m + 1, :] for m in range(TOGETHER)]
+            before = [big[pl.ds(place, 1), :] for place in places]
+            for m in range(TOGETHER):
+                total = before[m] + added[m]
+                for k in range(m):
+                    total = total + jnp.where(places[k] == places[m], added[k], 0.0)
+                before[m] = total
+            for m in range(TOGETHER):
+                big[pl.ds(places[m], 1), :] = before[m]
         return carry
 
-    lax.fori_loop(0, chunks, zero_step, 0)
-
-    def scatter_step(r, carry):
-        base = pl.multiple_of(r * group, group)
-        wrow = wref[pl.ds(r, 1), :]
-        for m in range(group):
-            row = pl.ds(home[ids[base + m]], 1)
-            big[row, :] += members[pl.ds(base + m, 1), :]
-            wacc[row, :] += wrow
-        return carry
-
-    lax.fori_loop(0, entries // group, scatter_step, 0)
+    lax.fori_loop(0, groups, scatter_step, 0)
 
     def put(i, slot):
         rows = pl.ds(pl.multiple_of(i * CHUNK, CHUNK), CHUNK)
@@ -147,7 +167,7 @@
             put(i - 2, slot).wait()
 
         rows = pl.ds(pl.multiple_of(i * CHUNK, CHUNK), CHUNK)
-        stage[slot] = big[rows, :].astype(jnp.bfloat16)
+        stage[slot] = big[rows, :width].astype(jnp.bfloat16)
         put(i, slot).start()
         return carry
 
@@ -159,7 +179,7 @@
     def weight_step(i, carry):
         rows = pl.ds(pl.multiple_of(i * LANES, LANES), LANES)
         wsum[pl.ds(i, 1), :] = jnp.sum(
-            jnp.where(lane == sub, wacc[rows, :], 0.0), axis=0, keepdims=True
+            jnp.where(lane == sub, big[rows, width:], 0.0), axis=0, keepdims=True
         )
         return carry
 
@@ -168,9 +188,9 @@
         put(i, i % 2).wait()
 
 
-def phase(second, home, ids, sigma, tables, table, group, coeffs=None):
+def phase(second, places, sigma, tables, table, group, coeffs=None):
     cubes, width = table.shape
-    entries = ids.shape[0]
+    entries = places[-1].shape[0]
     vmem = pl.BlockSpec(memory_space=pltpu.VMEM)
     smem = pl.BlockSpec(memory_space=pltpu.SMEM)
     anywhere = pl.BlockSpec(memory_space=pltpu.HBM)
@@ -180,26 +200,24 @@
         jax.ShapeDtypeStruct((cubes // LANES, LANES), jnp.float32),
     ]
     out_specs = [anywhere, vmem]
-    in_specs = [smem, smem] + [vmem] * 5
-    args = [home, ids, sigma, *tables]
+    in_specs = [smem] * len(places) + [vmem] * 5
+    args = [*places, sigma, *tables]
     if second:
         in_specs = in_specs + [vmem, anywhere]
         args = args + [coeffs, table]
     else:
         in_specs = in_specs + [anywhere]
         args = args + [table]
-        outs = [held] + outs
-        out_specs = [vmem] + out_specs
+        outs = [held, jax.ShapeDtypeStruct((entries,), jnp.int32)] + outs
+        out_specs = [vmem, smem] + out_specs
     return pl.pallas_call(
         functools.partial(kernel, second, group),
         out_shape=outs,
         in_specs=in_specs,
         out_specs=out_specs,
         scratch_shapes=[
-            pltpu.VMEM((cubes, width), jnp.float32),
-            pltpu.VMEM((entries, width), jnp.float32),
-            pltpu.VMEM((cubes, LANES), jnp.float32),
-            pltpu.VMEM((entries // group, LANES), jnp.float32),
+            pltpu.VMEM((cubes, width + LANES), jnp.float32),
+            pltpu.VMEM((entries // group, group, width + LANES), jnp.float32),
             pltpu.VMEM((2, CHUNK, width), jnp.bfloat16),
             pltpu.SemaphoreType.DMA((2,)),
         ],
@@ -486,10 +504,10 @@
     ids = matches.reshape(-1)
     sigma = sigma_coef[None, :]
     table = gather_all(noisy, grid)
-    coeffs, acc, wsum = phase(False, cube_home, ids, sigma, tables, table, group)
+    coeffs, rows, acc, wsum = phase(False, (cube_home, ids), sigma, tables, table, group)
     basic = settle(acc, wsum, noisy, grid)
     guide = gather_all(basic, grid)
-    acc2, wsum2 = phase(True, cube_home, ids, sigma, tables, guide, group, coeffs)
+    acc2, wsum2 = phase(True, (rows,), sigma, tables, guide, group, coeffs)
     return basic, settle(acc2, wsum2, noisy, grid)
 
 

time: 285 us -> 271 us (0.951)
  Pallas kernels: 277 us -> 262 us
    pallas_call x2, Pallas kernels: 88.6 us -> 74.5 us  [phase(): pl.pallas_call(functools.partial(kernel, second, group), out_shape=outs,...]
where the time goes in v2:
time: 271 us; the launch traced here: 267 us
  Pallas kernels  262 us (97%)
  local copies, waits for them, and re-layouts  4.14 us (2%)
    pallas_call x2, Pallas kernels, settle(): pl.pallas_call(functools.partial(reduce_kernel, grid), out_shape=jax.Shap...  94.6 us
    pallas_call x2, Pallas kernels, gather_all(): pl.pallas_call(functools.partial(gather_kernel, grid), out_shape=jax.Shap...  93.3 us
    pallas_call x2, Pallas kernels, phase(): pl.pallas_call(functools.partial(kernel, second, group), out_shape=outs,...  74.5 us

profile of v2, /device:TPU:15, one launch (start us, length us, event | category | flops | bytes accessed | tf_op | source)
XLA Modules:
  0.0 267.2 jit_solution(6809536758836374198)
XLA Ops:
  0.6 0.8 copy.10
  1.4 0.7 reshape.25.refs_1_
  2.1 47.2 %spread.2 = bf16[16,512,512]{2,1,0:T(8,128)(2,1)} custom-call(bf16[512,512]{1,0:T(8,128)(2,1)} %noisy.3), custom_call_target="tpu_custom_call" | custom-call | tf_op jit(solution)/shard_map/spread/pallas_call | solution.py:346
  49.3 38.0 %shrink.1 = (f32[1536,512]{1,0:T(8,128)}, s32[1536]{0:T(1024)}, bf16[8192,512]{1,0:T(8,128)(2,1)}, f32[64,128]{1,0:T(8,128)}) custom-call(s32[8192]{0:T(1024)} %refs_0_.1, s32[1536]{0:T(1024)} %reshape.25.refs_1_, f32[1,512]{1,0:T(1,128)} %bitcast.13, bf16[512,512]{1,0:T(8,128)(2,1)} %constant.8.clone.refs_3_.refs_2_, ...), custom_call_target="tpu_custom_call" | custom-call | tf_op jit(solution)/shard_map/shrink/pallas_call | solution.py:213
  87.4 47.3 %settle.2.x = bf16[512,512]{1,0:T(8,128)(2,1)} custom-call(bf16[8,2,512,512]{3,2,1,0:T(8,128)(2,1)} %bitcast.10, f32[8,2,4,128]{3,2,1,0:T(4,128)} %bitcast.12, bf16[512,512]{1,0:T(8,128)(2,1)} %noisy.3), custom_call_target="tpu_custom_call" | custom-call | tf_op jit(solution)/shard_map/settle/pallas_call | solution.py:471
  134.7 46.1 %spread.3 = bf16[16,512,512]{2,1,0:T(8,128)(2,1)} custom-call(bf16[512,512]{1,0:T(8,128)(2,1)} %settle.2.x), custom_call_target="tpu_custom_call" | custom-call | tf_op jit(solution)/shard_map/spread/pallas_call | solution.py:346
  180.8 0.0 copy-start
  180.8 36.5 %wiener.1 = (bf16[8192,512]{1,0:T(8,128)(2,1)}, f32[64,128]{1,0:T(8,128)}) custom-call(s32[1536]{0:T(1024)} %get-tuple-element.10.refs_0_, f32[1,512]{1,0:T(1,128)} %bitcast.14, bf16[512,512]{1,0:T(8,128)(2,1)} %constant.8.clone.refs_3_.refs_2_, bf16[512,512]{1,0:T(8,128)(2,1)} %constant.9.clone.refs_4_.refs_3_, ...), custom_call_target="tpu_custom_call" | custom-call | tf_op jit(solution)/shard_map/wiener/pallas_call | solution.py:213
  217.2 47.3 %settle.3 = bf16[512,512]{1,0:T(8,128)(2,1)} custom-call(bf16[8,2,512,512]{3,2,1,0:T(8,128)(2,1)} %bitcast.9, f32[8,2,4,128]{3,2,1,0:T(4,128)} %bitcast.11, bf16[512,512]{1,0:T(8,128)(2,1)} %noisy.3), custom_call_target="tpu_custom_call" | custom-call | tf_op jit(solution)/shard_map/settle/pallas_call | solution.py:471
  264.5 0.0 copy-done
  264.6 0.8 copy.13
  265.4 1.9 copy.14
Async XLA Ops:
  180.8 83.8 %copy-start = (bf16[512,512]{1,0:T(8,128)(2,1)S(1)}, bf16[512,512]{1,0:T(8,128)(2,1)}, u32[]{:S(2)}) copy-start(bf16[512,512]{1,0:T(8,128)(2,1)} %settle.2.x) | copy-start | bytes 1572868

commit v3 on v2

--- a/solution.py
+++ b/solution.py
@@ -14,6 +14,7 @@
 CHUNK = 512
 ROWS = 384
 TOGETHER = 2
+LAG = 3
 
 
 def dct_matrix(length):
@@ -55,51 +56,15 @@
 
 
 def kernel(second, group, *refs):
-    if second:
-        (rows_in, sigma, cube, cube_t, mix, mix_t, coeffs, table, acc_out, wsum) = refs[:10]
-    else:
-        (home, ids, sigma, cube, cube_t, mix, mix_t, table, coeffs, rows_in, acc_out, wsum) = refs[:12]
+    rows_in, sigma, cube, cube_t, mix, mix_t, taken_in, coeffs, acc_out, wsum = refs[:10]
     big, members, stage, sem = refs[-4:]
-    cubes, width = table.shape
+    cubes, width = acc_out.shape
     full = big.shape[1]
     groups = members.shape[0]
     entries = groups * group
     chunks = cubes // CHUNK
     steps = entries // ROWS
 
-    def fetch(i, slot):
-        rows = pl.ds(pl.multiple_of(i * CHUNK, CHUNK), CHUNK)
-        return pltpu.make_async_copy(table.at[rows, :], stage.at[slot], sem.at[slot])
-
-    fetch(0, 0).start()
-
-    def load_step(i, carry):
-        slot = lax.rem(i, 2)
-
-        @pl.when(i + 1 < chunks)
-        def _():
-            fetch(i + 1, 1 - slot).start()
-
-        fetch(i, slot).wait()
-        rows = pl.ds(pl.multiple_of(i * CHUNK, CHUNK), CHUNK)
-        big[rows, :width] = stage[slot].astype(jnp.float32)
-        return carry
-
-    lax.fori_loop(0, chunks, load_step, 0)
-
-    def gather_step(r, carry):
-        base = r * group
-        places = [rows_in[base + m] if second else home[ids[base + m]] for m in range(group)]
-        if not second:
-            for m in range(group):
-                rows_in[base + m] = places[m]
-        picked = [big[pl.ds(places[m], 1), :] for m in range(group)]
-        for m in range(group):
-            members[r, m : m + 1, :] = picked[m]
-        return carry
-
-    lax.fori_loop(0, groups, gather_step, 0)
-
     noise = sigma[...] * sigma[...]
     level = (shrink_level * sigma[...]) * (shrink_level * sigma[...])
 
@@ -107,12 +72,11 @@
         rows = pl.ds(pl.multiple_of(b * ROWS, ROWS), ROWS)
         refs_here = ROWS // group
         some = pl.ds(b * refs_here, refs_here)
-        taken = members[some, :, :width].reshape(ROWS, width).astype(jnp.bfloat16)
         cleared = cubes // steps
         big[pl.ds(pl.multiple_of(b * cleared, cleared), cleared), :] = jnp.zeros(
             (cleared, full), jnp.float32
         )
-        spec = jnp.dot(taken, cube_t[...], preferred_element_type=jnp.float32)
+        spec = jnp.dot(taken_in[rows, :], cube_t[...], preferred_element_type=jnp.float32)
         own = mix_rows(mix[...], spec)
         square = own * own
         if second:
@@ -188,28 +152,24 @@
         put(i, i % 2).wait()
 
 
-def phase(second, places, sigma, tables, table, group, coeffs=None):
-    cubes, width = table.shape
-    entries = places[-1].shape[0]
+def phase(second, places, sigma, tables, taken, cubes, group, coeffs=None):
+    entries, width = taken.shape
     vmem = pl.BlockSpec(memory_space=pltpu.VMEM)
     smem = pl.BlockSpec(memory_space=pltpu.SMEM)
-    anywhere = pl.BlockSpec(memory_space=pltpu.HBM)
     held = jax.ShapeDtypeStruct((entries, width), jnp.float32)
     outs = [
         jax.ShapeDtypeStruct((cubes, width), jnp.bfloat16),
         jax.ShapeDtypeStruct((cubes // LANES, LANES), jnp.float32),
     ]
-    out_specs = [anywhere, vmem]
-    in_specs = [smem] * len(places) + [vmem] * 5
-    args = [*places, sigma, *tables]
+    out_specs = [pl.BlockSpec(memory_space=pltpu.HBM), vmem]
+    in_specs = [smem] + [vmem] * 6
+    args = [places, sigma, *tables, taken]
     if second:
-        in_specs = in_specs + [vmem, anywhere]
-        args = args + [coeffs, table]
+        in_specs = in_specs + [vmem]
+        args = args + [coeffs]
     else:
-        in_specs = in_specs + [anywhere]
-        args = args + [table]
-        outs = [held, jax.ShapeDtypeStruct((entries,), jnp.int32)] + outs
-        out_specs = [vmem, smem] + out_specs
+        outs = [held] + outs
+        out_specs = [vmem] + out_specs
     return pl.pallas_call(
         functools.partial(kernel, second, group),
         out_shape=outs,
@@ -276,8 +236,15 @@
     )
 
 
-def gather_kernel(grid, x, out, send, recv, give, take, own):
-    count, held = out.shape[:2]
+def gather_kernel(grid, second, *refs):
+    if second:
+        x, places, taken = refs[:3]
+    else:
+        x, home, ids, taken, places = refs[:5]
+    held_in, big, members, send, recv, give, take = refs[-7:]
+    count, held = held_in.shape[:2]
+    groups, group = members.shape[:2]
+    width = x.shape[1]
     pieces = held // LANES
     ring = Ring(grid, count)
     orders = hops(ring.chips, pieces)
@@ -286,7 +253,11 @@
     ring.greet()
 
     def part(block, j):
-        return out.at[block, pl.ds(j * LANES, LANES), :]
+        return held_in.at[block, pl.ds(j * LANES, LANES), :]
+
+    def widen(block, j, source):
+        rows = pl.ds(pl.multiple_of(block * held + j * LANES, LANES), LANES)
+        big[rows, :] = source[...].astype(jnp.float32)
 
     started = []
 
@@ -307,9 +278,19 @@
                         ring.sides[way],
                     )
                 )
-    keep = pltpu.make_async_copy(x, out.at[ring.me], own.at[0])
-    keep.start()
-    start(remote(x, out.at[ring.me], give.at[0, last], take.at[0, last], ring.partner))
+    start(remote(x, held_in.at[ring.me], give.at[0, last], take.at[0, last], ring.partner))
+    for j in range(pieces):
+        widen(ring.me, j, x.at[pl.ds(j * LANES, LANES), :])
+    other = ring.me + 1 - 2 * ring.core
+
+    def accept(t):
+        for way in range(2):
+            d, j = orders[way][t]
+            block = ring.device(-d if way == 0 else d, 1 - ring.core)
+            piece = part(block, j)
+            remote(piece, piece, give.at[way, t], take.at[way, t], ring.partner).wait_recv()
+            widen(block, j, piece)
+
     for t in range(last):
         for way in range(2):
             d, j = orders[way][t]
@@ -324,41 +305,77 @@
                     )
                 )
             start(remote(piece, piece, give.at[way, t], take.at[way, t], ring.partner))
-    other = ring.me + 1 - 2 * ring.core
-    remote(
-        out.at[other], out.at[other], give.at[0, last], take.at[0, last], ring.partner
-    ).wait_recv()
-    for t in range(last):
-        for way in range(2):
-            d, j = orders[way][t]
-            piece = part(ring.device(-d if way == 0 else d, 1 - ring.core), j)
-            remote(piece, piece, give.at[way, t], take.at[way, t], ring.partner).wait_recv()
+            widen(block, j, piece)
+        if t == 2:
+            remote(
+                held_in.at[other], held_in.at[other], give.at[0, last], take.at[0, last], ring.partner
+            ).wait_recv()
+            for j in range(pieces):
+                widen(other, j, part(other, j))
+        if t >= LAG:
+            accept(t - LAG)
+    for t in range(last - LAG, last):
+        accept(t)
+
+    def gather_step(r, carry):
+        base = r * group
+        spots = [places[base + m] if second else home[ids[base + m]] for m in range(group)]
+        if not second:
+            for m in range(group):
+                places[base + m] = spots[m]
+        picked = [big[pl.ds(spots[m], 1), :] for m in range(group)]
+        for m in range(group):
+            members[r, m : m + 1, :] = picked[m]
+        return carry
+
+    lax.fori_loop(0, groups, gather_step, 0)
+
+    def narrow_step(b, carry):
+        some = LANES // group
+        rows = pl.ds(pl.multiple_of(b * LANES, LANES), LANES)
+        taken[rows, :] = members[pl.ds(b * some, some)].reshape(LANES, width).astype(taken.dtype)
+        return carry
+
+    lax.fori_loop(0, groups * group // LANES, narrow_step, 0)
     for copy in started:
         copy.wait_send()
-    keep.wait()
-
-
-def gather_all(x, grid):
+
+
+def gather_rows(x, lists, grid, groups, group):
     count = lax.axis_size("space")
     held, width = x.shape
+    entries = groups * group
     last = len(hops(count // 2, held // LANES)[0])
     sems = pltpu.SemaphoreType.DMA
-    out = pl.pallas_call(
-        functools.partial(gather_kernel, grid),
-        out_shape=jax.ShapeDtypeStruct((count, held, width), x.dtype),
-        in_specs=[pl.BlockSpec(memory_space=pltpu.VMEM)],
-        out_specs=pl.BlockSpec(memory_space=pltpu.HBM),
+    second = len(lists) == 1
+    vmem = pl.BlockSpec(memory_space=pltpu.VMEM)
+    smem = pl.BlockSpec(memory_space=pltpu.SMEM)
+    outs = [jax.ShapeDtypeStruct((entries, width), x.dtype)]
+    out_specs = [vmem]
+    if not second:
+        outs.append(jax.ShapeDtypeStruct((entries,), jnp.int32))
+        out_specs.append(smem)
+    return pl.pallas_call(
+        functools.partial(gather_kernel, grid, second),
+        out_shape=outs,
+        in_specs=[vmem] + [smem] * len(lists),
+        out_specs=out_specs,
         scratch_shapes=[
+            pltpu.VMEM((count, held, width), x.dtype),
+            pltpu.VMEM((count * held, width), jnp.float32),
+            pltpu.VMEM((groups, group, width), jnp.float32),
             sems((2, last)),
             sems((2, last)),
             sems((2, last + 1)),
             sems((2, last + 1)),
-            sems((1,)),
         ],
-        compiler_params=pltpu.CompilerParams(collective_id=0, has_side_effects=True),
+        compiler_params=pltpu.CompilerParams(
+            collective_id=2 if second else 0,
+            has_side_effects=True,
+            vmem_limit_bytes=60 * 1024 * 1024,
+        ),
         name="spread",
-    )(x)
-    return out.reshape(count * held, width)
+    )(x, *lists)
 
 
 def reduce_kernel(grid, acc, wsum, noisy, out, own, other, got, sent, wother, wgot, wsent, *sems):
@@ -499,15 +516,15 @@
 
 
 def body(grid, noisy, matches, cube_home, sigma_coef):
-    group = matches.shape[1]
+    groups, group = matches.shape
+    cubes = cube_home.shape[0]
     tables = make_tables(group)
-    ids = matches.reshape(-1)
     sigma = sigma_coef[None, :]
-    table = gather_all(noisy, grid)
-    coeffs, rows, acc, wsum = phase(False, (cube_home, ids), sigma, tables, table, group)
+    members, rows = gather_rows(noisy, (cube_home, matches.reshape(-1)), grid, groups, group)
+    coeffs, acc, wsum = phase(False, rows, sigma, tables, members, cubes, group)
     basic = settle(acc, wsum, noisy, grid)
-    guide = gather_all(basic, grid)
-    acc2, wsum2 = phase(True, (rows,), sigma, tables, guide, group, coeffs)
+    (guide,) = gather_rows(basic, (rows,), grid, groups, group)
+    acc2, wsum2 = phase(True, rows, sigma, tables, guide, cubes, group, coeffs)
     return basic, settle(acc2, wsum2, noisy, grid)
 
 

time: 271 us -> 252 us (0.930)
  Pallas kernels: 262 us -> 244 us
    pallas_call x2, Pallas kernels: 74.5 us -> 47.4 us  [phase(): pl.pallas_call(functools.partial(kernel, second, group), out_shape=outs,...]
    pallas_call x2, Pallas kernels: 93.3 us -> 104 us  [gather_rows(): pl.pallas_call(functools.partial(gather_kernel, grid, second), out_shape=...]
where the time goes in v3:
time: 252 us; the launch traced here: 249 us
  Pallas kernels  244 us (97%)
  local copies, waits for them, and re-layouts  4.14 us (2%)
    pallas_call x2, Pallas kernels, gather_rows(): pl.pallas_call(functools.partial(gather_kernel, grid, second), out_shape=...  104 us
    pallas_call x2, Pallas kernels, settle(): pl.pallas_call(functools.partial(reduce_kernel, grid), out_shape=jax.Shap...  92.2 us
    pallas_call x2, Pallas kernels, phase(): pl.pallas_call(functools.partial(kernel, second, group), out_shape=outs,...  47.4 us

profile of v3, /device:TPU:15, one launch (start us, length us, event | category | flops | bytes accessed | tf_op | source)
XLA Modules:
  0.0 248.7 jit_solution(576686492085565027)
XLA Ops:
  0.6 0.8 copy.10
  1.4 0.7 reshape.19.refs_2_
  2.1 53.2 %spread.2 = (bf16[1536,512]{1,0:T(8,128)(2,1)}, s32[1536]{0:T(1024)}) custom-call(bf16[512,512]{1,0:T(8,128)(2,1)} %noisy.3, s32[8192]{0:T(1024)} %refs_1_.1, s32[1536]{0:T(1024)} %reshape.19.refs_2_), custom_call_target="tpu_custom_call" | custom-call | tf_op jit(solution)/shard_map/spread/pallas_call | solution.py:358
  55.3 23.8 %shrink.1 = (f32[1536,512]{1,0:T(8,128)}, bf16[8192,512]{1,0:T(8,128)(2,1)}, f32[64,128]{1,0:T(8,128)}) custom-call(s32[1536]{0:T(1024)} %get-tuple-element.9.refs_0_.refs_1_, f32[1,512]{1,0:T(1,128)} %bitcast.9, bf16[512,512]{1,0:T(8,128)(2,1)} %constant.8.clone.refs_2_, bf16[512,512]{1,0:T(8,128)(2,1)} %constant.9.clone.refs_3_, ...), custom_call_target="tpu_custom_call" | custom-call | tf_op jit(solution)/shard_map/shrink/pallas_call | solution.py:173
  79.2 46.1 %settle.2.refs_0_ = bf16[512,512]{1,0:T(8,128)(2,1)} custom-call(bf16[8,2,512,512]{3,2,1,0:T(8,128)(2,1)} %bitcast.6, f32[8,2,4,128]{3,2,1,0:T(4,128)} %bitcast.8, bf16[512,512]{1,0:T(8,128)(2,1)} %noisy.3), custom_call_target="tpu_custom_call" | custom-call | tf_op jit(solution)/shard_map/settle/pallas_call | solution.py:488
  125.3 51.0 %spread.3.refs_6_ = bf16[1536,512]{1,0:T(8,128)(2,1)} custom-call(bf16[512,512]{1,0:T(8,128)(2,1)} %settle.2.refs_0_, s32[1536]{0:T(1024)} %get-tuple-element.9.refs_0_.refs_1_), custom_call_target="tpu_custom_call" | custom-call | tf_op jit(solution)/shard_map/spread/pallas_call | solution.py:358
  176.3 23.6 %wiener.1 = (bf16[8192,512]{1,0:T(8,128)(2,1)}, f32[64,128]{1,0:T(8,128)}) custom-call(s32[1536]{0:T(1024)} %get-tuple-element.9.refs_0_.refs_1_, f32[1,512]{1,0:T(1,128)} %bitcast.10, bf16[512,512]{1,0:T(8,128)(2,1)} %constant.8.clone.refs_2_, bf16[512,512]{1,0:T(8,128)(2,1)} %constant.9.clone.refs_3_, bf16[128,256]{1,0:T(8,128)(2,1)} %constant.10.clone.refs_4_, ...), custom_call_target="tpu_custom_call" | custom-call | tf_op jit(solution)/shard_map/wiener/pallas_call | solution.py:173
  199.9 0.0 copy-start
  199.9 46.1 %settle.3 = bf16[512,512]{1,0:T(8,128)(2,1)} custom-call(bf16[8,2,512,512]{3,2,1,0:T(8,128)(2,1)} %bitcast.5, f32[8,2,4,128]{3,2,1,0:T(4,128)} %bitcast.7, bf16[512,512]{1,0:T(8,128)(2,1)} %noisy.3), custom_call_target="tpu_custom_call" | custom-call | tf_op jit(solution)/shard_map/settle/pallas_call | solution.py:488
  246.1 0.0 copy-done
  246.1 0.8 copy.13
  246.9 1.9 copy.14
Async XLA Ops:
  199.9 46.2 %copy-start = (bf16[512,512]{1,0:T(8,128)(2,1)S(1)}, bf16[512,512]{1,0:T(8,128)(2,1)}, u32[]{:S(2)}) copy-start(bf16[512,512]{1,0:T(8,128)(2,1)} %settle.2.refs_0_) | copy-start | bytes 1572868

commit v4 on v3

--- a/solution.py
+++ b/solution.py
@@ -117,7 +117,7 @@
                 big[pl.ds(places[m], 1), :] = before[m]
         return carry
 
-    lax.fori_loop(0, groups, scatter_step, 0)
+    lax.fori_loop(0, groups, scatter_step, 0, unroll=2)
 
     def put(i, slot):
         rows = pl.ds(pl.multiple_of(i * CHUNK, CHUNK), CHUNK)
@@ -147,7 +147,7 @@
         )
         return carry
 
-    lax.fori_loop(0, cubes // LANES, weight_step, 0)
+    lax.fori_loop(0, cubes // LANES, weight_step, 0, unroll=4)
     for i in (chunks - 2, chunks - 1):
         put(i, i % 2).wait()
 
@@ -328,7 +328,7 @@
             members[r, m : m + 1, :] = picked[m]
         return carry
 
-    lax.fori_loop(0, groups, gather_step, 0)
+    lax.fori_loop(0, groups, gather_step, 0, unroll=2)
 
     def narrow_step(b, carry):
         some = LANES // group

time: 252 us -> 251 us (level)
  no operation moved by 1% of the time
where the time goes in v4:
time: 251 us; the launch traced here: 247 us
  Pallas kernels  242 us (96%)
  local copies, waits for them, and re-layouts  4.14 us (2%)
    pallas_call x2, Pallas kernels, gather_rows(): pl.pallas_call(functools.partial(gather_kernel, grid, second), out_shape=...  104 us
    pallas_call x2, Pallas kernels, settle(): pl.pallas_call(functools.partial(reduce_kernel, grid), out_shape=jax.Shap...  92.3 us
    pallas_call x2, Pallas kernels, phase(): pl.pallas_call(functools.partial(kernel, second, group), out_shape=outs,...  46.4 us

profile of v4, /device:TPU:15, one launch (start us, length us, event | category | flops | bytes accessed | tf_op | source)
XLA Modules:
  0.0 247.3 jit_solution(8433422179197715173)
XLA Ops:
  0.6 0.8 copy.10
  1.4 0.7 reshape.19.refs_2_
  2.1 52.9 %spread.2 = (bf16[1536,512]{1,0:T(8,128)(2,1)}, s32[1536]{0:T(1024)}) custom-call(bf16[512,512]{1,0:T(8,128)(2,1)} %noisy.3, s32[8192]{0:T(1024)} %refs_1_.1, s32[1536]{0:T(1024)} %reshape.19.refs_2_), custom_call_target="tpu_custom_call" | custom-call | tf_op jit(solution)/shard_map/spread/pallas_call | solution.py:358
  55.0 23.2 %shrink.1 = (f32[1536,512]{1,0:T(8,128)}, bf16[8192,512]{1,0:T(8,128)(2,1)}, f32[64,128]{1,0:T(8,128)}) custom-call(s32[1536]{0:T(1024)} %get-tuple-element.9.refs_0_.refs_1_, f32[1,512]{1,0:T(1,128)} %bitcast.9, bf16[512,512]{1,0:T(8,128)(2,1)} %constant.8.clone.refs_2_, bf16[512,512]{1,0:T(8,128)(2,1)} %constant.9.clone.refs_3_, ...), custom_call_target="tpu_custom_call" | custom-call | tf_op jit(solution)/shard_map/shrink/pallas_call | solution.py:173
  78.3 46.1 %settle.2.refs_0_ = bf16[512,512]{1,0:T(8,128)(2,1)} custom-call(bf16[8,2,512,512]{3,2,1,0:T(8,128)(2,1)} %bitcast.6, f32[8,2,4,128]{3,2,1,0:T(4,128)} %bitcast.8, bf16[512,512]{1,0:T(8,128)(2,1)} %noisy.3), custom_call_target="tpu_custom_call" | custom-call | tf_op jit(solution)/shard_map/settle/pallas_call | solution.py:488
  124.4 50.9 %spread.3.refs_6_ = bf16[1536,512]{1,0:T(8,128)(2,1)} custom-call(bf16[512,512]{1,0:T(8,128)(2,1)} %settle.2.refs_0_, s32[1536]{0:T(1024)} %get-tuple-element.9.refs_0_.refs_1_), custom_call_target="tpu_custom_call" | custom-call | tf_op jit(solution)/shard_map/spread/pallas_call | solution.py:358
  175.3 23.2 %wiener.1 = (bf16[8192,512]{1,0:T(8,128)(2,1)}, f32[64,128]{1,0:T(8,128)}) custom-call(s32[1536]{0:T(1024)} %get-tuple-element.9.refs_0_.refs_1_, f32[1,512]{1,0:T(1,128)} %bitcast.10, bf16[512,512]{1,0:T(8,128)(2,1)} %constant.8.clone.refs_2_, bf16[512,512]{1,0:T(8,128)(2,1)} %constant.9.clone.refs_3_, bf16[128,256]{1,0:T(8,128)(2,1)} %constant.10.clone.refs_4_, ...), custom_call_target="tpu_custom_call" | custom-call | tf_op jit(solution)/shard_map/wiener/pallas_call | solution.py:173
  198.5 0.0 copy-start
  198.5 46.1 %settle.3 = bf16[512,512]{1,0:T(8,128)(2,1)} custom-call(bf16[8,2,512,512]{3,2,1,0:T(8,128)(2,1)} %bitcast.5, f32[8,2,4,128]{3,2,1,0:T(4,128)} %bitcast.7, bf16[512,512]{1,0:T(8,128)(2,1)} %noisy.3), custom_call_target="tpu_custom_call" | custom-call | tf_op jit(solution)/shard_map/settle/pallas_call | solution.py:488
  244.6 0.0 copy-done
  244.6 0.8 copy.13
  245.4 1.9 copy.14
Async XLA Ops:
  198.5 46.2 %copy-start = (bf16[512,512]{1,0:T(8,128)(2,1)S(1)}, bf16[512,512]{1,0:T(8,128)(2,1)}, u32[]{:S(2)}) copy-start(bf16[512,512]{1,0:T(8,128)(2,1)} %settle.2.refs_0_) | copy-start | bytes 1572868
